TPU v7x, 512 devices: a whole 4x8x8 slice. The times are simulated.
512 devices in a mesh: energy: 8 (over y_lo, core), atom: 64 (over y_hi, x, z).
Axes of the slice: x: 4, y: 8 (y_hi: 2, y_lo: 4; y = y_hi * 4 + y_lo), z: 8, core: 2. Of those that a mesh axis runs over, the one named last changes fastest.
Arguments:
- green: bfloat16 [8, 64, 2, 512, 512], P('energy', 'atom'), may hold values from -0.25 to 0.25
- t_ref: bfloat16 [8, 64, 2, 32, 32], P('energy'), may hold values from -0.24748737 to 0.24748737
- radial: bfloat16 [8, 32, 1024], P('energy'), may hold values from -1 to 1
- energy_weight: float32 [8], P('energy'), may hold values from 10 to 60
- potential: float32 [64, 25, 1024], P('atom'), may hold values from -6 to 6
- coupling: float32 [25, 32], replicated, may hold values from -1 to 1
- zone: int32 [64, 15], P('atom'), may hold values from 0 to 63, as said below
- order: int32 [64], replicated, may hold values from 0 to 63, as said below
Outputs:
- mixed: float32 [64, 25, 1024], P('atom')
- final_density: float32 [64, 25, 1024], P('atom')
Inputs may be any that keep to these rules, and one draw needn't show every extreme that they name: `zone`: each row lists 16 - 1 distinct atom ids, none of them the atom at that row's position. `order`: A permutation of the atom ids.
All inputs are finite; a program needn't handle non-finite values.
Results may differ from a plain program's by a relative error of at most 0.035.
Values may be sent and summed in bfloat16 or wider, within the bound.
A program may use at most 64 MiB of HBM per device.

v0:
```python
import jax
import jax.numpy as jnp
from jax import lax
from jax.sharding import PartitionSpec as P

NITER = 4
MIXING = 0.5
STEEPNESS = 0.8


def drive_scale(field, basis, coupling):
    squares = basis.astype(jnp.float32) ** 2
    intersection = jnp.einsum("acr,br->acb", field, squares, precision=lax.Precision.HIGHEST)
    drive = jnp.einsum("acb,cb->ab", intersection, coupling, precision=lax.Precision.HIGHEST)
    return 1.0 + STEEPNESS * jnp.tanh(drive)


def scatter(zone_t, greens, channels):
    count = zone_t.shape[0]
    zone_size = zone_t.shape[1]
    order_size = zone_size * channels
    seed_block = jnp.concatenate([zone_t[:, 0, 0], zone_t[:, 0, 1]], -1).astype(jnp.float32)
    start = (
        jnp.zeros((count, zone_size, channels, 2 * channels), jnp.float32).at[:, 0].set(seed_block)
    )
    stacked = greens.reshape(count, 2 * order_size, order_size)
    iterate = start
    for sweep in range(NITER):
        current = iterate.astype(jnp.bfloat16).reshape(count, order_size, 2 * channels)
        product = jnp.einsum("aij,ajk->aik", stacked, current, preferred_element_type=jnp.float32)
        product = product.reshape(count, 2, zone_size, channels, 2 * channels)
        real_part = product[:, 0, :, :, :channels] - product[:, 1, :, :, channels:]
        imag_part = product[:, 0, :, :, channels:] + product[:, 1, :, :, :channels]
        scattered = jnp.concatenate([real_part, imag_part], -1).astype(jnp.bfloat16)
        left = jnp.einsum(
            "azbc,azcd->azbd", zone_t[:, :, 0], scattered, preferred_element_type=jnp.float32
        )
        right = jnp.einsum(
            "azbc,azcd->azbd", zone_t[:, :, 1], scattered, preferred_element_type=jnp.float32
        )
        update = jnp.concatenate(
            [
                left[..., :channels] - right[..., channels:],
                left[..., channels:] + right[..., :channels],
            ],
            -1,
        )
        iterate = start + update
    return iterate[:, 0, :, channels:]


def density(imag_tau, basis, coupling, weight):
    radial_f = basis.astype(jnp.float32)
    mixed_rows = jnp.einsum("aij,jr->air", imag_tau, radial_f, precision=lax.Precision.HIGHEST)
    paired = radial_f[None] * mixed_rows
    return weight * jnp.einsum("ci,air->acr", coupling, paired, precision=lax.Precision.HIGHEST)


def summed(local_terms):
    return lax.psum(local_terms, "energy")


def body(green, t_ref, radial, energy_weight, potential, coupling, zone, order):
    count = potential.shape[0]
    total = order.shape[0]
    channels = coupling.shape[1]
    atom_rank = lax.axis_index("atom")
    index_list = jnp.arange(total, dtype=jnp.int32)
    position_of = jnp.zeros((total,), jnp.int32).at[order].set(index_list)
    own_positions = atom_rank * count + jnp.arange(count, dtype=jnp.int32)
    zone_pos = jnp.concatenate([own_positions[:, None], position_of[zone]], 1)
    base_all = t_ref[0]
    base_own = lax.dynamic_slice_in_dim(base_all, atom_rank * count, count, 0)
    basis = radial[0]
    weight = energy_weight[0]
    greens = green[0]

    def matrices(field):
        scale = drive_scale(field, basis, coupling)
        own_t = (scale[:, None, :, None] * base_own.astype(jnp.float32)).astype(jnp.bfloat16)
        every = lax.all_gather(own_t, "atom", axis=0, tiled=True)
        return every[zone_pos]

    def path_blocks(field):
        return scatter(matrices(field), greens, channels)

    def one_pass(field):
        return density(path_blocks(field), basis, coupling, weight)

    first = one_pass(potential)
    mixed = (1.0 - MIXING) * potential + MIXING * summed(first)
    final = summed(one_pass(mixed))
    return (mixed, final)


def solution(mesh):
    placed = (
        P("energy", "atom", None, None, None),
        P("energy", None, None, None, None),
        P("energy", None, None),
        P("energy"),
        P("atom", None, None),
        P(),
        P("atom", None),
        P(),
    )
    return jax.shard_map(
        body,
        mesh=mesh,
        in_specs=placed,
        out_specs=(P("atom", None, None), P("atom", None, None)),
        check_vma=False,
    )
```

profile of v0, /device:TPU:2, one launch (start us, length us, event | category | flops | bytes accessed | tf_op | source)
XLA Modules:
  0.0 634.7 jit_solution(14289547260079247878)
XLA Ops:
  7.2 0.8 fusion.69
  8.0 0.7 compare_select_fusion.2
  8.7 1.2 fusion.3
  9.9 0.8 scatter_custom_fusion
  10.6 0.7 gather_fusion
  11.6 0.5 copy.92
  12.2 203.8 %all_gather.6 = bf16[64,2,32,32]{3,2,1,0:T(8,128)(2,1)S(1)} all-gather(bf16[1,2,32,32]{3,2,1,0:T(8,128)(2,1)S(1)} %fusion.43), channel_id=1, replica_groups=mesh['energy'=8,'atom'=64] {'atom'}, dimensions={0}, use_global_device_ids=true | all-gather | bytes 266240 | tf_op jit(solution)/shard_map/all_gather | solution.py:81
  215.9 0.6 gather_fusion.1
  216.7 0.4 convolution_bitcast_fusion.23
  217.8 0.2 convolution_bitcast_fusion.22
  218.4 0.4 convolution_bitcast_fusion.20
  220.2 0.4 convolution_bitcast_fusion.17
  222.0 0.4 convolution_bitcast_fusion.14
  224.2 0.6 copy-done.1
  224.8 0.3 convolution_multiply_fusion.3
  225.1 0.5 copy-done.4
  225.5 0.9 fusion.1
  226.5 96.0 %all-reduce.5.cloned.1.call-done = f32[1,25,1024]{2,1,0:T(8,128)} async-done(((f32[1,25,1024]{2,1,0:T(8,128)}), f32[1,25,1024]{2,1,0:T(8,128)}) %all-reduce.5.cloned.1.call-update) | async-done | bytes 102416 | tf_op jit(solution)/shard_map/psum | solution.py:60
  322.5 0.9 fusion.21
  323.5 0.3 fusion.4
  323.8 195.4 %all_gather.7 = bf16[64,2,32,32]{3,2,1,0:T(8,128)(2,1)S(1)} all-gather(bf16[1,2,32,32]{3,2,1,0:T(8,128)(2,1)S(1)} %fusion.44), channel_id=1, replica_groups=mesh['energy'=8,'atom'=64] {'atom'}, dimensions={0}, use_global_device_ids=true | all-gather | bytes 266240 | tf_op jit(solution)/shard_map/all_gather | solution.py:81
  519.3 0.6 gather_fusion.2
  520.0 0.4 convolution_bitcast_fusion.11
  520.9 0.2 convolution_bitcast_fusion.9
  521.8 0.4 convolution_bitcast_fusion.8
  523.5 0.4 convolution_bitcast_fusion.5
  525.3 0.4 convolution_bitcast_fusion.2
  526.9 0.3 convolution_multiply_fusion.2
  527.1 0.9 fusion
  528.0 0.7 copy.77
  528.8 97.4 %all-reduce.7.cloned.1.call-done = f32[1,25,1024]{2,1,0:T(8,128)} async-done(((f32[1,25,1024]{2,1,0:T(8,128)}), f32[1,25,1024]{2,1,0:T(8,128)}) %all-reduce.7.cloned.1.call-update) | async-done | bytes 102416 | tf_op jit(solution)/shard_map/psum | solution.py:60
  626.2 1.7 copy.78
  (79 shorter events, 10.2 us)
Async XLA Ops:
  7.2 209.5 %copy-start = (bf16[1,1,2,512,512]{4,3,2,1,0:T(8,128)(2,1)S(1)}, bf16[1,1,2,512,512]{4,3,2,1,0:T(8,128)(2,1)}, u32[]{:S(2)}) copy-start(bf16[1,1,2,512,512]{4,3,2,1,0:T(8,128)(2,1)} %param.12) | copy-start | bytes 3145732
  7.2 4.2 copy-start.3
  7.2 315.3 %all-reduce.5.cloned.1.call-start = ((), (), s32[]{:S(2)}) async-start(), calls=%async_computation | async-start | bytes 262144 | tf_op jit(solution)/shard_map/psum | solution.py:60
  224.0 0.8 copy-start.1
  224.8 0.7 copy-start.4
  226.4 96.1 %copy-start.2 = (f32[1,25,1024]{2,0,1:T(1,128)S(1)}, f32[1,25,1024]{2,0,1:T(1,128)}, u32[]{:S(2)}) copy-start(f32[1,25,1024]{2,0,1:T(1,128)} %param.16) | copy-start | bytes 307204
  226.4 399.8 %all-reduce.7.cloned.1.call-start = ((), (), s32[]{:S(2)}) async-start(), calls=%async_computation.1 | async-start | bytes 262144 | tf_op jit(solution)/shard_map/psum | solution.py:60
Sparse Core Ops, SparseCore 0:
  226.6 95.9 all-reduce.4
  528.2 98.0 all-reduce.6
where the time goes:
time: 635 us
  blocking collectives  399 us (63%)
  waiting for transfers between devices  193 us (30%)
  between operations  15.2 us (2%)
  matrix products  11 us (2%)
  local copies, waits for them, and re-layouts  8.5 us (1%)
  other arithmetic  7.25 us (1%)
    all_gather x2, blocking collectives, matrices(): every = lax.all_gather(own_t, 'atom', axis=0, tiled=True)  399 us
    psum x2, waiting for transfers between devices, summed(): return lax.psum(local_terms, 'energy')  193 us
  transfers between devices with their start and end apart: 2, of which 2 were waited for; matrix products, arithmetic and copies ran while one was open for 0% of the time, Pallas kernels for 0%

commit v1 on v0

--- a/solution.py
+++ b/solution.py
@@ -78,7 +78,9 @@
     def matrices(field):
         scale = drive_scale(field, basis, coupling)
         own_t = (scale[:, None, :, None] * base_own.astype(jnp.float32)).astype(jnp.bfloat16)
-        every = lax.all_gather(own_t, "atom", axis=0, tiled=True)
+        every = jnp.concatenate(
+            lax.all_to_all(jnp.stack([own_t] * lax.axis_size("atom")), "atom", 0, 0), axis=0
+        )
         return every[zone_pos]
 
     def path_blocks(field):

time: 635 us -> 243 us (0.38)
  blocking collectives: 399 us -> 27.3 us
  waiting for transfers between devices: 193 us -> 150 us
  starting transfers between devices: 0.08 us -> 19.2 us
    all_gather x2 -> x0, blocking collectives: 399 us -> none  [matrices(): every = lax.all_gather(own_t, 'atom', axis=0, tiled=True)]
    psum x2, waiting for transfers between devices: 193 us -> 138 us  [summed(): return lax.psum(local_terms, 'energy')]
    all_to_all x0 -> x1, blocking collectives: none -> 27.3 us  [matrices(): lax.all_to_all(jnp.stack([own_t] * lax.axis_size('atom')), 'atom', 0, 0)]
    all_to_all x0 -> x1, starting transfers between devices: none -> 19.1 us  [matrices(): lax.all_to_all(jnp.stack([own_t] * lax.axis_size('atom')), 'atom', 0, 0)]
    all_to_all x0 -> x1, waiting for transfers between devices: none -> 11.9 us  [matrices(): lax.all_to_all(jnp.stack([own_t] * lax.axis_size('atom')), 'atom', 0, 0)]
  transfers between devices with their start and end apart: 2 -> 3, of which waited for: 2 -> 3; matrix products, arithmetic and copies ran while one was open for 0% -> 1% of each run, Pallas kernels for 0% -> 0%
where the time goes in v1:
time: 243 us; the launch traced here: 242 us
  waiting for transfers between devices  150 us (62%)
  blocking collectives  27.3 us (11%)
  starting transfers between devices  19.2 us (8%)
  between operations  15.2 us (6%)
  local copies, waits for them, and re-layouts  13.8 us (6%)
  matrix products  11.2 us (5%)
  other arithmetic  5.82 us (2%)
    psum x2, waiting for transfers between devices, summed(): return lax.psum(local_terms, 'energy')  138 us
    all_to_all x1, blocking collectives, matrices(): lax.all_to_all(jnp.stack([own_t] * lax.axis_size('atom')), 'atom', 0, 0)  27.3 us
    all_to_all x1, starting transfers between devices, matrices(): lax.all_to_all(jnp.stack([own_t] * lax.axis_size('atom')), 'atom', 0, 0)  19.1 us
    all_to_all x1, waiting for transfers between devices, matrices(): lax.all_to_all(jnp.stack([own_t] * lax.axis_size('atom')), 'atom', 0, 0)  11.9 us
    unnamed x19, local copies, waits for them, and re-layouts  7.65 us
  transfers between devices with their start and end apart: 3, of which 3 were waited for; matrix products, arithmetic and copies ran while one was open for 1% of the time, Pallas kernels for 0%

profile of v1, /device:TPU:2, one launch (start us, length us, event | category | flops | bytes accessed | tf_op | source)
XLA Modules:
  0.0 242.3 jit_solution(16881262846047828272)
XLA Ops:
  7.2 1.2 fusion.3
  8.4 1.3 constant_dynamic-slice_fusion
  9.7 0.5 copy.92
  10.5 1.7 reshape.838
  12.2 19.1 %all-to-all-start = ((bf16[64,2,1024]{2,1,0:T(2,128)(2,1)}), bf16[64,2,1024]{2,1,0:T(2,128)(2,1)S(1)}, u32[]{:S(2)}, u32[]{:S(2)}) async-start(bf16[64,2,1024]{2,1,0:T(2,128)(2,1)} %reshape.838), calls=%async_computation | async-start | bytes 524288 | tf_op jit(solution)/shard_map/all_to_all | solution.py:82
  32.1 0.8 scatter_custom_fusion
  32.9 0.7 gather_fusion
  33.6 11.9 %all-to-all-done = bf16[64,2,1024]{2,1,0:T(2,128)(2,1)S(1)} async-done(((bf16[64,2,1024]{2,1,0:T(2,128)(2,1)}), bf16[64,2,1024]{2,1,0:T(2,128)(2,1)S(1)}, u32[]{:S(2)}, u32[]{:S(2)}) %all-to-all-start) | async-done | bytes 262176 | tf_op jit(solution)/shard_map/all_to_all | solution.py:82
  45.5 0.5 reshape.839
  46.0 0.6 gather_fusion.1
  46.8 0.4 convolution_bitcast_fusion.23
  48.5 0.4 convolution_bitcast_fusion.20
  50.3 0.4 convolution_bitcast_fusion.17
  52.1 0.4 convolution_bitcast_fusion.14
  53.7 0.6 copy-done.1
  54.5 0.4 copy-done.3
  55.0 0.9 fusion.1
  56.0 69.5 %all-reduce.5.cloned.1.call-done = f32[1,25,1024]{2,1,0:T(8,128)} async-done(((f32[1,25,1024]{2,1,0:T(8,128)}), f32[1,25,1024]{2,1,0:T(8,128)}) %all-reduce.5.cloned.1.call-update) | async-done | bytes 102416 | tf_op jit(solution)/shard_map/psum | solution.py:60
  125.5 0.9 fusion.21
  126.4 0.3 fusion.4
  127.1 1.0 reshape.840
  128.1 27.3 %all_to_all.10 = bf16[64,2,1024]{2,1,0:T(2,128)(2,1)S(1)} all-to-all(bf16[64,2,1024]{2,1,0:T(2,128)(2,1)S(1)} %reshape.840), channel_id=1, replica_groups=mesh['energy'=8,'atom'=64] {'atom'}, dimensions={0} | all-to-all | bytes 524288 | tf_op jit(solution)/shard_map/all_to_all | solution.py:82
  155.4 0.5 reshape.841
  155.9 0.6 gather_fusion.2
  156.6 0.4 convolution_bitcast_fusion.11
  158.4 0.4 convolution_bitcast_fusion.8
  160.2 0.4 convolution_bitcast_fusion.5
  161.9 0.4 convolution_bitcast_fusion.2
  163.8 0.9 fusion
  164.7 0.7 copy.77
  165.4 68.3 %all-reduce.7.cloned.1.call-done = f32[1,25,1024]{2,1,0:T(8,128)} async-done(((f32[1,25,1024]{2,1,0:T(8,128)}), f32[1,25,1024]{2,1,0:T(8,128)}) %all-reduce.7.cloned.1.call-update) | async-done | bytes 102416 | tf_op jit(solution)/shard_map/psum | solution.py:60
  233.8 1.7 copy.78
  (88 shorter events, 11.6 us)
Async XLA Ops:
  7.2 39.6 %copy-start = (bf16[1,1,2,512,512]{4,3,2,1,0:T(8,128)(2,1)S(1)}, bf16[1,1,2,512,512]{4,3,2,1,0:T(8,128)(2,1)}, u32[]{:S(2)}) copy-start(bf16[1,1,2,512,512]{4,3,2,1,0:T(8,128)(2,1)} %param.12) | copy-start | bytes 3145732
  12.2 33.3 %all-to-all-start = ((bf16[64,2,1024]{2,1,0:T(2,128)(2,1)}), bf16[64,2,1024]{2,1,0:T(2,128)(2,1)S(1)}, u32[]{:S(2)}, u32[]{:S(2)}) async-start(bf16[64,2,1024]{2,1,0:T(2,128)(2,1)} %reshape.838), calls=%async_computation | async-start | bytes 524288 | tf_op jit(solution)/shard_map/all_to_all | solution.py:82
  31.3 0.7 copy-start.4
  31.3 94.2 %all-reduce.5.cloned.1.call-start = ((), (), s32[]{:S(2)}) async-start(), calls=%async_computation.2 | async-start | bytes 262144 | tf_op jit(solution)/shard_map/psum | solution.py:60
  32.1 0.8 copy-start.5
  53.4 0.8 copy-start.1
  54.3 0.7 copy-start.3
  55.9 69.6 %copy-start.2 = (f32[1,25,1024]{2,0,1:T(1,128)S(1)}, f32[1,25,1024]{2,0,1:T(1,128)}, u32[]{:S(2)}) copy-start(f32[1,25,1024]{2,0,1:T(1,128)} %param.16) | copy-start | bytes 307204
  55.9 177.9 %all-reduce.7.cloned.1.call-start = ((), (), s32[]{:S(2)}) async-start(), calls=%async_computation.3 | async-start | bytes 262144 | tf_op jit(solution)/shard_map/psum | solution.py:60
Sparse Core Ops, SparseCore 0:
  56.1 69.3 all-reduce.4
  164.8 68.9 all-reduce.6

commit v2 on v0

--- a/solution.py
+++ b/solution.py
@@ -57,7 +57,7 @@
 
 
 def summed(local_terms):
-    return lax.psum(local_terms, "energy")
+    return jnp.sum(lax.all_gather(local_terms, "energy"), axis=0)
 
 
 def body(green, t_ref, radial, energy_weight, potential, coupling, zone, order):

time: 635 us -> 514 us (0.81)
  the two profiles are of different devices: /device:TPU:2 before, /device:TPU:1 now
where the time goes in v2:
time: 514 us
  blocking collectives  488 us (95%)
  matrix products  9.79 us (2%)
  local copies, waits for them, and re-layouts  8 us (2%)
  other arithmetic  6.45 us (1%)
    all_gather x2, blocking collectives, matrices(): every = lax.all_gather(own_t, 'atom', axis=0, tiled=True)  399 us
    all_gather x2, blocking collectives, summed(): return jnp.sum(lax.all_gather(local_terms, 'energy'), axis=0)  89.3 us

profile of v2, /device:TPU:1, one launch (start us, length us, event | category | flops | bytes accessed | tf_op | source)
XLA Modules:
  0.0 514.2 jit_solution(17348661613996198498)
XLA Ops:
  1.4 0.4 copy-done
  1.9 0.7 fusion.71
  2.5 0.7 compare_select_fusion.2
  3.2 1.2 fusion.3
  4.4 0.8 scatter_custom_fusion
  5.2 0.7 gather_fusion
  6.2 0.5 copy.84
  6.7 208.1 %all_gather.18 = bf16[64,2,32,32]{3,2,1,0:T(8,128)(2,1)S(1)} all-gather(bf16[1,2,32,32]{3,2,1,0:T(8,128)(2,1)S(1)} %fusion.45), channel_id=1, replica_groups=mesh['energy'=8,'atom'=64] {'atom'}, dimensions={0}, use_global_device_ids=true | all-gather | bytes 266240 | tf_op jit(solution)/shard_map/all_gather | solution.py:81
  214.9 0.6 gather_fusion.1
  215.6 0.4 convolution_bitcast_fusion.23
  216.5 0.2 convolution_bitcast_fusion.21
  216.7 0.2 convolution_bitcast_fusion.22
  217.4 0.4 convolution_bitcast_fusion.20
  219.1 0.4 convolution_bitcast_fusion.17
  220.9 0.4 convolution_bitcast_fusion.14
  222.5 0.6 copy-done.1
  223.1 0.3 convolution_multiply_fusion.3
  223.4 0.2 fusion.1
  223.6 44.9 %all-gather = f32[8,25,1024]{2,1,0:T(8,128)S(1)} all-gather(f32[1,25,1024]{2,1,0:T(8,128)S(1)} %fusion.1), channel_id=2, replica_groups=mesh['energy'=8,'atom'=64] {'energy'}, dimensions={0}, use_global_device_ids=true | all-gather | bytes 921600 | tf_op jit(solution)/shard_map/all_gather | solution.py:60
  268.6 0.8 copy-done.2
  269.5 0.3 fusion.4
  269.8 0.4 copy-done.3
  270.3 190.7 %all_gather.21 = bf16[64,2,32,32]{3,2,1,0:T(8,128)(2,1)S(1)} all-gather(bf16[1,2,32,32]{3,2,1,0:T(8,128)(2,1)S(1)} %fusion.46), channel_id=1, replica_groups=mesh['energy'=8,'atom'=64] {'atom'}, dimensions={0}, use_global_device_ids=true | all-gather | bytes 266240 | tf_op jit(solution)/shard_map/all_gather | solution.py:81
  460.9 0.6 gather_fusion.2
  461.7 0.4 convolution_bitcast_fusion.11
  463.4 0.4 convolution_bitcast_fusion.8
  465.2 0.4 convolution_bitcast_fusion.5
  467.0 0.4 convolution_bitcast_fusion.2
  468.5 0.3 convolution_multiply_fusion.2
  468.8 0.2 fusion
  469.0 44.4 %all-gather.1 = f32[8,25,1024]{2,1,0:T(8,128)S(1)} all-gather(f32[1,25,1024]{2,1,0:T(8,128)S(1)} %fusion), channel_id=3, replica_groups=mesh['energy'=8,'atom'=64] {'energy'}, dimensions={0}, use_global_device_ids=true | all-gather | bytes 921600 | tf_op jit(solution)/shard_map/all_gather | solution.py:60
  513.5 0.7 reduce_sum.25
  (78 shorter events, 10.4 us)
Async XLA Ops:
  0.6 1.2 copy-start
  0.6 2.5 copy-start.5
  0.7 5.3 %copy-start.4 = (bf16[1,64,2,32,32]{1,4,3,2,0:T(8,128)(2,1)S(1)}, bf16[1,64,2,32,32]{1,4,3,2,0:T(8,128)(2,1)}, u32[]{:S(2)}) copy-start(bf16[1,64,2,32,32]{1,4,3,2,0:T(8,128)(2,1)} %param.13) | copy-start | bytes 786436
  222.2 0.8 copy-start.1
  268.5 0.9 copy-start.2
  269.5 0.6 copy-start.3
